TPU v7x, 32 devices: a whole 2x2x4 slice. The times are simulated.
32 devices in a mesh: dom: 8 (over z, y), tm: 4 (over x, core).
Axes of the slice: x: 2, y: 2, z: 4, core: 2. Of those that a mesh axis runs over, the one named last changes fastest.
Arguments:
- panel_signal: bfloat16 [8, 8192], P('tm', 'dom'), may hold values from -6 to 6
- panel_box: int32 [8192], P('dom'), may hold values from 0 to 15
- radiation: bfloat16 [8192, 1024], P('dom'), may hold values from -0.75 to 0.75
- reception: bfloat16 [8192, 1024], P('dom'), may hold values from -0.1875 to 0.1875
- translation: bfloat16 [64, 8, 1024], P(None, None, 'dom'), may hold values from -1 to 1
- list_source: int32 [128, 8], replicated, may hold values from 0 to 127
- list_class: int32 [128, 8], replicated, may hold values from 0 to 63
- list_count: int32 [128], replicated, may hold values from 1 to 8, as said below
Outputs:
- panel_field: bfloat16 [8, 8192], P('tm', 'dom')
Inputs may be any that keep to these rules, and one draw needn't show every extreme that they name: `panel_box`: indices a panel's box among the 16 boxes of its own index of dom. Box a uses the first list_count[a] entries of its lists; the rest are padding.
All inputs are finite; a program needn't handle non-finite values.
Results may differ from a plain program's by a relative error of at most 0.0057.
Values may be sent and summed in bfloat16 or wider, within the bound.
A program may use at most 64 MiB of HBM per device.

v0:
```python
import math

import jax
import jax.numpy as jnp
from jax import lax
from jax.sharding import PartitionSpec as P

BOX_DEV = 16
J = 8


def lag_sum(kern_rows, gathered, out_steps, offset):
    entries = kern_rows.shape[0]
    lags_all = kern_rows.shape[1]
    width = kern_rows.shape[2]
    results = []
    for step_out in range(out_steps):
        total = jnp.zeros((entries, width), jnp.float32)
        for step_in in range(gathered.shape[1]):
            delay = offset + step_out - step_in
            picked = lax.dynamic_index_in_dim(
                kern_rows, jnp.clip(delay, 0, lags_all - 1), 1, keepdims=False
            )
            weight = jnp.where(delay >= 0, picked.astype(jnp.float32), 0.0)
            total = total + weight * gathered[:, step_in].astype(jnp.float32)
        results.append(total)
    return jnp.stack(results, axis=1)


def body(
    panel_signal, panel_box, radiation, reception, translation, list_source, list_class, list_count
):
    rows_own = panel_signal.shape[0]
    dirs_own = translation.shape[2]
    boxes_all = list_source.shape[0]
    classes_all = translation.shape[0]
    lags_all = translation.shape[1]
    box_onehot = (panel_box[None, :] == jnp.arange(BOX_DEV, dtype=jnp.int32)[:, None]).astype(
        jnp.bfloat16
    )
    used_rows = (jnp.arange(J, dtype=jnp.int32)[None, :] < list_count[:, None]).astype(jnp.bfloat16)
    block_size = math.gcd(boxes_all, 256)

    def translate_all(table, rays, out_steps, offset):
        width = table.shape[2]
        count_in = rays.shape[1]
        flat_table = table.reshape(classes_all, lags_all * width)
        flat_rays = rays.reshape(boxes_all, count_in * width)

        def one_block(index):
            sources = lax.dynamic_slice_in_dim(
                list_source, index * block_size, block_size, 0
            ).reshape(block_size * J)
            classes = lax.dynamic_slice_in_dim(
                list_class, index * block_size, block_size, 0
            ).reshape(block_size * J)
            keep_rows = lax.dynamic_slice_in_dim(
                used_rows, index * block_size, block_size, 0
            ).reshape(block_size * J, 1)
            kern_rows = (jnp.take(flat_table, classes, axis=0) * keep_rows).reshape(
                block_size * J, lags_all, width
            )
            gathered = jnp.take(flat_rays, sources, axis=0).reshape(block_size * J, count_in, width)
            summed = lag_sum(kern_rows, gathered, out_steps, offset)
            return jnp.sum(summed.reshape(block_size, J, out_steps, width), axis=1)

        blocks = lax.map(one_block, jnp.arange(boxes_all // block_size, dtype=jnp.int32))
        return blocks.reshape(boxes_all, out_steps, width)

    masked = panel_signal[:, None, :] * box_onehot[None]
    outgoing = jnp.einsum(
        "rbp,pk->brk", masked, radiation, preferred_element_type=jnp.float32
    ).astype(jnp.bfloat16)
    spread = lax.all_to_all(outgoing, "dom", split_axis=2, concat_axis=0, tiled=True)
    first = lax.axis_index("tm") * rows_own
    empty = jnp.zeros((boxes_all, rows_own, dirs_own), jnp.float32)
    piece = lax.all_gather(spread, "tm", axis=1, tiled=True)

    def active():
        return empty + translate_all(translation, piece, rows_own, first)

    def passive():
        return empty

    incoming = lax.cond(jnp.int32(0) <= first + rows_own - 1, active, passive)
    rays = lax.all_to_all(
        incoming.astype(jnp.bfloat16), "dom", split_axis=0, concat_axis=2, tiled=True
    )
    partial_value = jnp.einsum("brk,pk->brp", rays, reception, preferred_element_type=jnp.float32)
    field = jnp.sum(partial_value * box_onehot.astype(jnp.float32)[:, None, :], axis=0)
    return field.astype(jnp.bfloat16)


def solution(mesh):
    placed = (
        P("tm", "dom"),
        P("dom"),
        P("dom", None),
        P("dom", None),
        P(None, None, "dom"),
        P(),
        P(),
        P(),
    )
    return jax.shard_map(
        body, mesh=mesh, in_specs=placed, out_specs=P("tm", "dom"), check_vma=False
    )
```

profile of v0, /device:TPU:0, one launch (start us, length us, event | category | flops | bytes accessed | tf_op | source)
XLA Modules:
  0.0 77.4 jit_solution(18071585750592534816)
XLA Ops:
  0.0 0.0 copy-start
  0.0 0.0 copy-start.4
  0.0 0.8 %fusion.37 = (f32[16,1024]{1,0:T(8,128)S(1)}, bf16[16,1024]{1,0:T(8,128)(2,1)S(1)}) fusion(s32[1024]{0:T(1024)} %param.11), kind=kLoop, calls=%fused_computation.71 | loop fusion | flops 49152 | bytes 102400 | tf_op jit(solution)/shard_map/convert_element_type | solution.py:90
  0.9 0.8 copy-done
  1.6 0.0 copy-start.1
  1.6 0.0 copy-start.2
  1.6 0.0 copy-start.3
  1.6 1.2 %fusion.29 = bf16[16,2,1024]{2,0,1:T(8,128)(2,1)S(1)} fusion(bf16[1024,1024]{1,0:T(8,128)(2,1)S(1)} %copy-done, bf16[16,1024]{1,0:T(8,128)(2,1)S(1)} %get-tuple-element.91, bf16[2,1024]{1,0:T(2,128)(2,1)} %param.10), kind=kOutput, calls=%fused_computation.61 | convolution fusion | flops 67174400 | bytes 2199552 | tf_op jit(solution)/shard_map/rbp,pk->brk/dot_general | solution.py:71
  2.8 0.4 copy.42
  3.2 1.2 %reshape.173 = bf16[8,2,2048]{2,1,0:T(2,128)(2,1)} reshape(bf16[1024,2,16]{2,1,0:T(2,128)(2,1)S(1)} %bitcast.51) | data formatting | bytes 131072
  4.4 7.3 %all-to-all-start = ((bf16[8,2,2048]{2,1,0:T(2,128)(2,1)}), bf16[8,2,2048]{2,1,0:T(2,128)(2,1)S(1)}, u32[]{:S(2)}, u32[]{:S(2)}) async-start(bf16[8,2,2048]{2,1,0:T(2,128)(2,1)} %reshape.173), calls=%async_computation | async-start | bytes 131072 | tf_op jit(solution)/shard_map/all_to_all | solution.py:74
  11.7 0.0 copy-done.4
  11.7 0.1 fusion.33
  11.8 6.8 %all-to-all-done = bf16[8,2,2048]{2,1,0:T(2,128)(2,1)S(1)} async-done(((bf16[8,2,2048]{2,1,0:T(2,128)(2,1)}), bf16[8,2,2048]{2,1,0:T(2,128)(2,1)S(1)}, u32[]{:S(2)}, u32[]{:S(2)}) %all-to-all-start) | async-done | bytes 65568 | tf_op jit(solution)/shard_map/all_to_all | solution.py:74
  18.6 0.4 reshape.174
  19.0 0.3 copy.43
  19.3 5.8 %all_gather.3 = bf16[128,8,128]{2,0,1:T(8,128)(2,1)S(1)} all-gather(bf16[128,2,128]{2,0,1:T(8,128)(2,1)S(1)} %bitcast.53), channel_id=1, replica_groups=mesh['dom'=8,'tm'=4] {'tm'}, dimensions={1}, use_global_device_ids=true | all-gather | bytes 327680 | tf_op jit(solution)/shard_map/all_gather | solution.py:77
  25.1 0.0 copy-done.1
  25.1 0.0 copy-done.2
  25.1 0.0 copy-done.3
  25.1 39.9 %conditional.1 = (bf16[128,2,128]{2,0,1:T(8,128)(2,1)S(1)}) conditional(s32[]{:T(128)} %convert_element_type.158, () %tuple.13, (s32[]{:T(128)}, s32[128,8]{0,1:T(8,128)S(1)}, bf16[64,8,128]{2,1,0:T(8,128)(2,1)S(1)}, bf16[128,8]{1,0:T(8,128)(2,1)S(1)}, s32[128,8]{0,1:T(8,128)S(1)}, /*index=5*/bf16[128,8,128]{2,0,1:T(8,128)(2,1)S(1)}) %tuple.27), branch_computations={%region_0.0_spmd, %region_1.3_spmd} | conditional | flops 13881379 | bytes 45001176 | solution.py:85
  25.1 0.1 copy.45
  25.2 0.1 reshape.154
  25.3 0.1 copy.44
  25.4 0.1 reshape.151
  25.6 5.3 %gather_fusion = bf16[1024,1024]{1,0:T(8,128)(2,1)} fusion(bf16[64,1024]{1,0:T(8,128)(2,1)S(1)} %bitcast.48, s32[1024]{0:T(1024)S(1)} %broadcast_clamp_fusion.1), kind=kCustom, calls=%fused_computation | custom fusion | bytes 4198400 | tf_op jit(solution)/shard_map/cond/branch_1_fun/while/body/eval_jaxpr/jit(_take)/gather | solution.py:60
  30.9 3.9 %copy.38 = bf16[1024,1024]{0,1:T(8,128)(2,1)} copy(bf16[1024,1024]{1,0:T(8,128)(2,1)} %gather_fusion) | data formatting | bytes 4194304 | tf_op jit(solution)/shard_map/cond/branch_1_fun/while/body/eval_jaxpr/jit(_take)/gather | solution.py:60
  34.8 3.9 %copy.39 = bf16[1024,8,128]{2,0,1:T(8,128)(2,1)} copy(bf16[1024,8,128]{0,2,1:T(8,128)(2,1)} %bitcast.49) | data formatting | bytes 4194304 | tf_op jit(solution)/shard_map/cond/branch_1_fun/while/body/eval_jaxpr/jit(_take)/gather | solution.py:60
  38.7 0.1 reshape.152
  38.8 0.1 reshape.149
  38.9 0.1 mul.98
  39.0 3.3 %select_multiply_fusion = bf16[1024,8,128]{2,0,1:T(8,128)(2,1)} fusion(bf16[1024,8,128]{2,0,1:T(8,128)(2,1)} %copy.39, pred[1024]{0:T(1024)(128)(4,1)S(1)} %get-tuple-element.89, bf16[1024]{0:T(1024)(128)(2,1)S(1)} %mul.98), kind=kLoop, calls=%fused_computation.2 | loop fusion | flops 2097152 | bytes 4197376 | tf_op jit(solution)/shard_map/cond/branch_1_fun/while/body/eval_jaxpr/mul | solution.py:60
  42.4 5.4 %gather_fusion.1 = bf16[1024,1024]{1,0:T(8,128)(2,1)} fusion(bf16[128,1024]{1,0:T(8,128)(2,1)S(1)} %copy_bitcast_fusion, s32[1024]{0:T(1024)S(1)} %broadcast_clamp_fusion), kind=kCustom, calls=%fused_computation.1 | custom fusion | bytes 4198400 | tf_op jit(solution)/shard_map/cond/branch_1_fun/while/body/eval_jaxpr/jit(_take)/gather | solution.py:63
  47.7 3.9 %copy.40 = bf16[1024,1024]{0,1:T(8,128)(2,1)} copy(bf16[1024,1024]{1,0:T(8,128)(2,1)} %gather_fusion.1) | data formatting | bytes 4194304 | tf_op jit(solution)/shard_map/cond/branch_1_fun/while/body/eval_jaxpr/jit(_take)/gather | solution.py:63
  51.7 3.9 %copy.41 = bf16[1024,8,128]{2,0,1:T(8,128)(2,1)} copy(bf16[1024,8,128]{0,2,1:T(8,128)(2,1)} %bitcast.50) | data formatting | bytes 4194304 | tf_op jit(solution)/shard_map/cond/branch_1_fun/while/body/eval_jaxpr/jit(_take)/gather | solution.py:63
  55.6 3.2 %broadcast_select_fusion = bf16[1024,8,128]{2,0,1:T(8,128)(2,1)} fusion(bf16[1024,8,128]{2,0,1:T(8,128)(2,1)} %copy.41, pred[1024]{0:T(1024)(128)(4,1)S(1)} %get-tuple-element.88), kind=kLoop, calls=%fused_computation.3 | loop fusion | flops 1048576 | bytes 4195328 | tf_op jit(solution)/shard_map/cond/branch_1_fun/while/body/eval_jaxpr/jit(_take)/select_n | solution.py:63
  58.7 3.0 %fusion.15 = f32[128,8,1,128]{3,1,0,2:T(8,128)S(1)} fusion(bf16[1024,8,128]{2,0,1:T(8,128)(2,1)} %select_multiply_fusion, s32[]{:T(128)S(6)} %min.50, pred[]{:T(512)S(6)} %ge.70, pred[]{:T(512)S(6)} %ge.68, pred[]{:T(512)S(6)} %ge.67, pred[]{:T(512)S(6)} %ge.66, pred[]{:T(512)S(6)} %ge.65, pred[]{:T(512)S(6)} %ge.64, pred[]{:T(512)S(6)} %ge.63, pred[]{:T(512)S(6)} %ge.60, ...), kind=kLoop, calls=%fused_computation.36 | loop fusion | flops 5111808 | bytes 4718632 | tf_op jit(solution)/shard_map/cond/branch_1_fun/while/body/eval_jaxpr/stack | solution.py:27
  61.7 3.0 %fusion.7 = f32[128,8,1,128]{3,1,0,2:T(8,128)S(1)} fusion(bf16[1024,8,128]{2,0,1:T(8,128)(2,1)} %select_multiply_fusion, s32[]{:T(128)S(6)} %min.49, pred[]{:T(512)S(6)} %ge.69, pred[]{:T(512)S(6)} %ge.68, pred[]{:T(512)S(6)} %ge.67, pred[]{:T(512)S(6)} %ge.66, pred[]{:T(512)S(6)} %ge.65, pred[]{:T(512)S(6)} %ge.64, pred[]{:T(512)S(6)} %ge.63, pred[]{:T(512)S(6)} %ge.60, ...), kind=kLoop, calls=%fused_computation.28 | loop fusion | flops 5111808 | bytes 4718632 | tf_op jit(solution)/shard_map/cond/branch_1_fun/while/body/eval_jaxpr/stack | solution.py:27
  64.8 0.3 maximum_reduce_fusion
  65.0 0.1 copy.55
  65.1 9.3 %all_to_all.36 = bf16[128,2,128]{2,1,0:T(2,128)(2,1)S(1)} all-to-all(bf16[128,2,128]{2,1,0:T(2,128)(2,1)S(1)} %copy.55), channel_id=1, replica_groups=mesh['dom'=8,'tm'=4] {'dom'}, dimensions={0} | all-to-all | bytes 131072 | tf_op jit(solution)/shard_map/all_to_all | solution.py:86
  74.5 2.9 %fusion.26 = bf16[2,1024]{1,0:T(2,128)(2,1)} fusion(bf16[16,2,1024]{2,0,1:T(8,128)(2,1)S(1)} %all_to_all.33, bf16[1024,1024]{1,0:T(8,128)(2,1)} %param.13, f32[16,1024]{1,0:T(8,128)S(1)} %get-tuple-element.90), kind=kOutput, calls=%fused_computation.60 | convolution fusion | flops 67172352 | bytes 2232320 | tf_op jit(solution)/shard_map/brk,pk->brp/dot_general | solution.py:89
  (8 shorter events, 0.1 us)
Async XLA Ops:
  0.0 1.6 %copy-start = (bf16[1024,1024]{1,0:T(8,128)(2,1)S(1)}, bf16[1024,1024]{1,0:T(8,128)(2,1)}, u32[]{:S(2)}) copy-start(bf16[1024,1024]{1,0:T(8,128)(2,1)} %param.12) | copy-start | bytes 6291460
  0.0 11.7 %copy-start.4 = (s32[128]{0:T(128)S(1)}, s32[128]{0:T(128)}, u32[]{:S(2)}) copy-start(s32[128]{0:T(128)} %param.17) | copy-start | bytes 1540
  1.6 23.5 %copy-start.1 = (bf16[64,8,128]{2,1,0:T(8,128)(2,1)S(1)}, bf16[64,8,128]{2,1,0:T(8,128)(2,1)}, u32[]{:S(2)}) copy-start(bf16[64,8,128]{2,1,0:T(8,128)(2,1)} %param.14) | copy-start | bytes 393220
  1.6 23.5 %copy-start.2 = (s32[128,8]{0,1:T(8,128)S(1)}, s32[128,8]{0,1:T(8,128)}, u32[]{:S(2)}) copy-start(s32[128,8]{0,1:T(8,128)} %param.16) | copy-start | bytes 12292
  1.6 23.5 %copy-start.3 = (s32[128,8]{0,1:T(8,128)S(1)}, s32[128,8]{0,1:T(8,128)}, u32[]{:S(2)}) copy-start(s32[128,8]{0,1:T(8,128)} %param.15) | copy-start | bytes 12292
  4.4 14.2 %all-to-all-start = ((bf16[8,2,2048]{2,1,0:T(2,128)(2,1)}), bf16[8,2,2048]{2,1,0:T(2,128)(2,1)S(1)}, u32[]{:S(2)}, u32[]{:S(2)}) async-start(bf16[8,2,2048]{2,1,0:T(2,128)(2,1)} %reshape.173), calls=%async_computation | async-start | bytes 131072 | tf_op jit(solution)/shard_map/all_to_all | solution.py:74
where the time goes:
time: 78 us; the launch traced here: 77.4 us
  local copies, waits for them, and re-layouts  30.3 us (39%)
  blocking collectives  15.1 us (19%)
  other arithmetic  13.7 us (18%)
  starting transfers between devices  7.31 us (9%)
  waiting for transfers between devices  6.81 us (9%)
  matrix products  4.12 us (5%)
    gather x3, local copies, waits for them, and re-layouts, one_block(): jnp.take(flat_rays, sources, axis=0)  13.2 us
    gather x3, local copies, waits for them, and re-layouts, one_block(): jnp.take(flat_table, classes, axis=0) * keep_rows  13.2 us
    all_to_all x1, blocking collectives, body(): lax.all_to_all(incoming.astype(jnp.bfloat16), 'dom', split_axis=0, concat...  9.29 us
    all_to_all x1, starting transfers between devices, body(): lax.all_to_all(outgoing, 'dom', split_axis=2, concat_axis=0, tiled=True)  7.31 us
    all_to_all x1, waiting for transfers between devices, body(): lax.all_to_all(outgoing, 'dom', split_axis=2, concat_axis=0, tiled=True)  6.81 us
    another operation x2, other arithmetic, lag_sum(): return jnp.stack(results, axis=1)  6.01 us
    all_gather x1, blocking collectives, body(): piece = lax.all_gather(spread, 'tm', axis=1, tiled=True)  5.78 us
    mul x1, other arithmetic, one_block(): jnp.take(flat_table, classes, axis=0) * keep_rows  3.27 us
  transfers between devices with their start and end apart: 1, of which 1 were waited for; matrix products, arithmetic and copies ran while one was open for 0% of the time, Pallas kernels for 0%

commit v1 on v0

--- a/solution.py
+++ b/solution.py
@@ -1,13 +1,12 @@
+import functools
 import math
 
 import jax
 import jax.numpy as jnp
 from jax import lax
+from jax.experimental import pallas as pl
+from jax.experimental.pallas import tpu as pltpu
 from jax.sharding import PartitionSpec as P
-
-BOX_DEV = 16
-J = 8
-
 
 def lag_sum(kern_rows, gathered, out_steps, offset):
     entries = kern_rows.shape[0]
@@ -35,6 +34,8 @@
     boxes_all = list_source.shape[0]
     classes_all = translation.shape[0]
     lags_all = translation.shape[1]
+    BOX_DEV = boxes_all // lax.axis_size("dom")
+    J = list_source.shape[1]
     box_onehot = (panel_box[None, :] == jnp.arange(BOX_DEV, dtype=jnp.int32)[:, None]).astype(
         jnp.bfloat16
     )
@@ -91,6 +92,352 @@
     return field.astype(jnp.bfloat16)
 
 
+LANES = 128
+SUBLANES = 8
+MESH = pl.DeviceIdType.MESH
+
+
+def pick_lanes(parts, lane_group):
+    total = parts[0]
+    for index in range(1, len(parts)):
+        total = jnp.where(lane_group == index, parts[index], total)
+    return total
+
+
+def spin(values, shift):
+    shift = shift % LANES
+    return values if shift == 0 else pltpu.roll(values, shift, 1)
+
+
+def kernel(
+    n_dom,
+    n_tm,
+    signal_ref,
+    box_ref,
+    rad_hbm,
+    rec_hbm,
+    trans_hbm,
+    source_ref,
+    class_ref,
+    count_ref,
+    out_ref,
+    rad,
+    rec,
+    trans,
+    trans_wide,
+    kern,
+    rays,
+    send_out,
+    recv_out,
+    send_in,
+    recv_in,
+    rows_tmp,
+    load_sem,
+    out_send_sem,
+    out_recv_sem,
+    in_send_sem,
+    in_recv_sem,
+):
+    n_dev = n_dom * n_tm
+    dom, tm = lax.axis_index("dom"), lax.axis_index("tm")
+    me = dom * n_tm + tm
+    steps_own, panels = signal_ref.shape
+    dirs_all = rad.shape[1]
+    classes, lags, _ = trans.shape
+    entries = source_ref.shape[0]
+    boxes_own = source_ref.shape[1] // n_dom
+    span = LANES // n_tm
+    pieces = boxes_own // n_tm
+    block = steps_own * pieces
+    rows_all = n_tm * block
+    halves = lags // n_tm
+    chunks = load_sem.shape[0] // 2 - 1
+    depth = panels // chunks
+
+    def place(peer):
+        return {"dom": lax.div(peer, n_tm), "tm": lax.rem(peer, n_tm)}
+
+    def rad_copy(index):
+        at = pl.ds(index * depth, depth)
+        return pltpu.make_async_copy(rad_hbm.at[at, :], rad.at[at, :], load_sem.at[index])
+
+    rec_copy = pltpu.make_async_copy(rec_hbm, rec, load_sem.at[chunks])
+    trans_copy = pltpu.make_async_copy(trans_hbm, trans, load_sem.at[chunks + 1])
+
+    for index in range(chunks):
+        rad_copy(index).start()
+    trans_copy.start()
+    rec_copy.start()
+
+    barrier = pltpu.get_barrier_semaphore()
+
+    def greet(offset, carry):
+        peer = lax.rem(me + offset, n_dev)
+        pl.semaphore_signal(barrier, inc=1, device_id=place(peer), device_id_type=MESH)
+        return carry
+
+    lax.fori_loop(1, n_dev, greet, 0)
+
+    lane_group = lax.broadcasted_iota(jnp.int32, (SUBLANES, LANES), 1) // span
+    sublane = lax.broadcasted_iota(jnp.int32, (SUBLANES, LANES), 0)
+
+    row = lax.broadcasted_iota(jnp.int32, (rows_all, panels), 0)
+    row_box = (row % pieces) * n_tm + row // block
+    owned = box_ref[...] == row_box
+    signal = signal_ref[...].astype(jnp.float32)
+    spread = signal[0:1]
+    row_step = (row // pieces) % steps_own
+    for step in range(1, steps_own):
+        spread = jnp.where(row_step == step, signal[step : step + 1], spread)
+    masked = jnp.where(owned, spread, 0.0).astype(jnp.bfloat16)
+
+    outgoing = jnp.zeros((rows_all, dirs_all), jnp.float32)
+    for index in range(chunks):
+        rad_copy(index).wait()
+        outgoing = outgoing + jnp.dot(
+            masked[:, index * depth : (index + 1) * depth],
+            rad[index * depth : (index + 1) * depth, :],
+            preferred_element_type=jnp.float32,
+        )
+    for owner in range(n_dom):
+        tiles = [
+            outgoing[part * block : (part + 1) * block, owner * LANES : (owner + 1) * LANES]
+            for part in range(n_tm)
+        ]
+        for time in range(n_tm):
+            moved = [spin(tiles[part], span * (part - time)) for part in range(n_tm)]
+            send_out[owner * n_tm + time] = pick_lanes(moved, lane_group).astype(jnp.bfloat16)
+
+    pl.semaphore_wait(barrier, n_dev - 1)
+
+    def out_copy(peer, slot):
+        return pltpu.make_async_remote_copy(
+            src_ref=send_out.at[peer],
+            dst_ref=recv_out.at[slot],
+            send_sem=out_send_sem.at[peer],
+            recv_sem=out_recv_sem.at[slot],
+            device_id=place(peer),
+            device_id_type=MESH,
+        )
+
+    def in_copy(peer, slot):
+        return pltpu.make_async_remote_copy(
+            src_ref=send_in.at[peer],
+            dst_ref=recv_in.at[slot],
+            send_sem=in_send_sem.at[peer],
+            recv_sem=in_recv_sem.at[slot],
+            device_id=place(peer),
+            device_id_type=MESH,
+        )
+
+    def send_first(offset, carry):
+        out_copy(lax.rem(me + offset, n_dev), me).start()
+        return carry
+
+    lax.fori_loop(1, n_dev, send_first, 0)
+    recv_out[me] = send_out[me]
+
+    trans_copy.wait()
+    trans_wide[...] = trans[...].astype(jnp.float32).reshape(classes * lags, LANES)
+    kern[classes] = jnp.zeros((halves, SUBLANES, LANES), jnp.float32)
+
+    def spread_class(index, carry):
+        base = index * (SUBLANES * lags)
+        for half in range(halves):
+            moved = []
+            for part in range(n_tm):
+                tile = trans_wide[pl.ds(base + half * n_tm + part, SUBLANES, stride=lags), :]
+                shift = lax.rem((part - tm + n_tm) * span, LANES)
+                moved.append(pltpu.roll(tile, shift, 1))
+            tile = pick_lanes(moved, lane_group)
+            for at in range(SUBLANES):
+                kern[index * SUBLANES + at, half] = jnp.broadcast_to(
+                    tile[at : at + 1], (SUBLANES, LANES)
+                )
+        return carry
+
+    lax.fori_loop(0, classes // SUBLANES, spread_class, 0)
+
+    def take_rays(step, carry):
+        owner = lax.rem(dom + step, n_dom)
+        for time in range(n_tm):
+            slot = owner * n_tm + time
+
+            @pl.when(slot != me)
+            def _():
+                out_copy(slot, slot).wait_recv()
+
+            rows_tmp[time * block : (time + 1) * block, :] = recv_out[slot].astype(jnp.float32)
+        for piece in range(pieces):
+            tile = rows_tmp[pl.ds(piece, SUBLANES, stride=pieces), :]
+            later = [tile]
+            for lag in range(1, n_tm):
+                later.append(jnp.where(sublane >= lag, pltpu.roll(tile, lag, 0), 0.0))
+            for part in range(n_tm):
+                moved = [spin(later[lag], span * (lag - part)) for lag in range(n_tm)]
+                rays[owner * boxes_own + piece * n_tm + part] = pick_lanes(moved, lane_group)
+        return carry
+
+    lax.fori_loop(0, n_dom, take_rays, 0)
+
+    def translate(step, carry):
+        owner = lax.rem(dom + step, n_dom)
+
+        def one_piece(piece, inner):
+            sums = []
+            for part in range(n_tm):
+                box = owner * boxes_own + piece * n_tm + part
+                used = count_ref[box]
+                totals = [jnp.zeros((SUBLANES, LANES), jnp.float32) for _ in range(halves)]
+                for entry in range(entries):
+                    kind = jnp.where(entry < used, class_ref[entry, box], classes)
+                    ray = rays[source_ref[entry, box]]
+                    for half in range(halves):
+                        totals[half] = totals[half] + kern[kind, half] * ray
+                total = totals[0]
+                for half in range(1, halves):
+                    late = half * n_tm
+                    total = total + jnp.where(
+                        sublane >= late, pltpu.roll(totals[half], late, 0), 0.0
+                    )
+                turn = LANES // 2
+                while turn >= span:
+                    total = total + pltpu.roll(total, turn, 1)
+                    turn //= 2
+                sums.append(total)
+            rows_tmp[pl.ds(piece, SUBLANES, stride=pieces), :] = pick_lanes(sums, lane_group)
+            return inner
+
+        lax.fori_loop(0, pieces, one_piece, 0)
+        for time in range(n_tm):
+            slot = owner * n_tm + time
+            send_in[slot] = rows_tmp[time * block : (time + 1) * block, :].astype(jnp.bfloat16)
+
+            @pl.when(slot != me)
+            def _():
+                in_copy(slot, me).start()
+
+        return carry
+
+    lax.fori_loop(1, n_dom + 1, translate, 0)
+    recv_in[me] = send_in[me]
+
+    rec_copy.wait()
+    field = jnp.zeros((rows_all, panels), jnp.float32)
+    for owner in range(n_dom):
+        tiles = []
+        for time in range(n_tm):
+            slot = owner * n_tm + time
+
+            @pl.when(slot != me)
+            def _():
+                in_copy(slot, slot).wait_recv()
+
+            tiles.append(recv_in[slot].astype(jnp.float32))
+        incoming = []
+        for part in range(n_tm):
+            moved = [spin(tiles[time], span * (time - part)) for time in range(n_tm)]
+            incoming.append(pick_lanes(moved, lane_group))
+        incoming = jnp.concatenate(incoming, axis=0).astype(jnp.bfloat16)
+        field = field + lax.dot_general(
+            incoming,
+            rec[:, owner * LANES : (owner + 1) * LANES],
+            (((1,), (1,)), ((), ())),
+            preferred_element_type=jnp.float32,
+        )
+    chosen = jnp.where(owned, field, 0.0)
+    for step in range(steps_own):
+        mine = jnp.where(row_step == step, chosen, 0.0)
+        out_ref[step : step + 1, :] = jnp.sum(mine, axis=0, keepdims=True).astype(out_ref.dtype)
+
+    def drain(offset, carry):
+        peer = lax.rem(me + offset, n_dev)
+        out_copy(peer, me).wait_send()
+        in_copy(peer, me).wait_send()
+        return carry
+
+    lax.fori_loop(1, n_dev, drain, 0)
+
+
+def fused_body(
+    n_dom,
+    n_tm,
+    panel_signal,
+    panel_box,
+    radiation,
+    reception,
+    translation,
+    list_source,
+    list_class,
+    list_count,
+):
+    steps_own, panels = panel_signal.shape
+    dirs_all = radiation.shape[1]
+    classes, lags, _ = translation.shape
+    boxes_all = list_source.shape[0]
+    n_dev = n_dom * n_tm
+    block = steps_own * (boxes_all // n_dom) // n_tm
+    chunks = 4
+    vmem = pl.BlockSpec(memory_space=pltpu.VMEM)
+    smem = pl.BlockSpec(memory_space=pltpu.SMEM)
+    hbm = pl.BlockSpec(memory_space=pl.ANY)
+    message = pltpu.VMEM((n_dev, block, LANES), jnp.bfloat16)
+    return pl.pallas_call(
+        functools.partial(kernel, n_dom, n_tm),
+        out_shape=jax.ShapeDtypeStruct((steps_own, panels), jnp.bfloat16),
+        in_specs=[vmem, vmem, hbm, hbm, hbm, smem, smem, smem],
+        out_specs=vmem,
+        scratch_shapes=[
+            pltpu.VMEM((panels, dirs_all), jnp.bfloat16),
+            pltpu.VMEM((panels, dirs_all), jnp.bfloat16),
+            pltpu.VMEM(translation.shape, jnp.bfloat16),
+            pltpu.VMEM((classes * lags, LANES), jnp.float32),
+            pltpu.VMEM((classes + 1, lags // n_tm, SUBLANES, LANES), jnp.float32),
+            pltpu.VMEM((boxes_all, SUBLANES, LANES), jnp.float32),
+            message,
+            message,
+            message,
+            message,
+            pltpu.VMEM((n_tm * block, LANES), jnp.float32),
+            pltpu.SemaphoreType.DMA((2 * chunks + 2,)),
+            pltpu.SemaphoreType.DMA((n_dev,)),
+            pltpu.SemaphoreType.DMA((n_dev,)),
+            pltpu.SemaphoreType.DMA((n_dev,)),
+            pltpu.SemaphoreType.DMA((n_dev,)),
+        ],
+        compiler_params=pltpu.CompilerParams(collective_id=0, has_side_effects=True),
+    )(
+        panel_signal,
+        panel_box.reshape(1, panels),
+        radiation,
+        reception,
+        translation,
+        list_source.T,
+        list_class.T,
+        list_count,
+    )
+
+
+def whole_body(n_dom, n_tm, *args):
+    panel_signal, translation, boxes_all = args[0], args[4], args[5].shape[0]
+    steps_own = panel_signal.shape[0]
+    classes, lags, dirs_own = translation.shape
+    boxes_own = boxes_all // n_dom
+    fits = (
+        dirs_own == LANES
+        and LANES % n_tm == 0
+        and lags == SUBLANES
+        and steps_own * n_tm == lags
+        and lags % n_tm == 0
+        and boxes_own % n_tm == 0
+        and steps_own * boxes_own == n_tm * SUBLANES
+        and classes % SUBLANES == 0
+    )
+    if fits:
+        return fused_body(n_dom, n_tm, *args)
+    return body(*args)
+
+
 def solution(mesh):
     placed = (
         P("tm", "dom"),
@@ -103,5 +450,6 @@
         P(),
     )
     return jax.shard_map(
-        body, mesh=mesh, in_specs=placed, out_specs=P("tm", "dom"), check_vma=False
-    )
+        functools.partial(whole_body, mesh.shape["dom"], mesh.shape["tm"]),
+        mesh=mesh, in_specs=placed, out_specs=P("tm", "dom"), check_vma=False
+    )

time: 78 us -> 26.6 us (0.34)
  local copies, waits for them, and re-layouts: 30.3 us -> 1.28 us
  Pallas kernels: 0 us -> 25.1 us
  blocking collectives: 15.1 us -> 0 us
  other arithmetic: 13.7 us -> 0 us
  starting transfers between devices: 7.31 us -> 0 us
  waiting for transfers between devices: 6.81 us -> 0 us
  matrix products: 4.12 us -> 0 us
    gather x6 -> x0, local copies, waits for them, and re-layouts: 26.4 us -> none  [the longest x3 13.2 us: one_block(): jnp.take(flat_rays, sources, axis=0)]
    pallas_call x0 -> x1, Pallas kernels: none -> 25.1 us  [fused_body(): pl.pallas_call(functools.partial(kernel, n_dom, n_tm), out_shape=jax.Shap...]
    all_to_all x1 -> x0, blocking collectives: 9.29 us -> none  [body(): lax.all_to_all(incoming.astype(jnp.bfloat16), 'dom', split_axis=0, concat...]
    all_to_all x1 -> x0, starting transfers between devices: 7.31 us -> none  [body(): lax.all_to_all(outgoing, 'dom', split_axis=2, concat_axis=0, tiled=True)]
    all_to_all x1 -> x0, waiting for transfers between devices: 6.81 us -> none  [body(): lax.all_to_all(outgoing, 'dom', split_axis=2, concat_axis=0, tiled=True)]
    another operation x2 -> x0, other arithmetic: 6.01 us -> none  [lag_sum(): return jnp.stack(results, axis=1)]
    all_gather x1 -> x0, blocking collectives: 5.78 us -> none  [body(): piece = lax.all_gather(spread, 'tm', axis=1, tiled=True)]
    dot_general x2 -> x0, matrix products: 4.12 us -> none  [the longest x1 2.93 us: body(): jnp.einsum('brk,pk->brp', rays, reception, preferred_element_type=jnp.flo...]
  transfers between devices with their start and end apart: 1 -> 0, of which waited for: 1 -> 0; matrix products, arithmetic and copies ran while one was open for 0% -> 0% of each run, Pallas kernels for 0% -> 0%
where the time goes in v1:
time: 26.6 us; the launch traced here: 26.4 us
  Pallas kernels  25.1 us (94%)
  local copies, waits for them, and re-layouts  1.28 us (5%)
    pallas_call x1, Pallas kernels, fused_body(): pl.pallas_call(functools.partial(kernel, n_dom, n_tm), out_shape=jax.Shap...  25.1 us
    unnamed x1, local copies, waits for them, and re-layouts  1.28 us

profile of v1, /device:TPU:0, one launch (start us, length us, event | category | flops | bytes accessed | tf_op | source)
XLA Modules:
  0.0 26.4 jit_solution(16538467021430258933)
XLA Ops:
  0.0 25.1 %shard_map.82 = bf16[2,1024]{1,0:T(2,128)(2,1)} custom-call(bf16[2,1024]{1,0:T(2,128)(2,1)} %signal_ref.1, s32[1,1024]{1,0:T(1,128)} %bitcast.3, bf16[1024,1024]{1,0:T(8,128)(2,1)} %rad_hbm.1, bf16[1024,1024]{1,0:T(8,128)(2,1)} %rec_hbm.1, bf16[64,8,128]{2,1,0:T(8,128)(2,1)} %trans_hbm.1, s32[8,128]{1,0:T(8,128)} %bitcast.4, s32[8,128]{1,0:T(8,128)} %bitcast.5, ...), custom_call_target="tpu_custom_call" | custom-call | tf_op jit(solution)/shard_map/pallas_call | solution.py:385
  25.1 1.3 %copy.10 = bf16[2,1024]{1,0:T(2,128)(2,1)} copy(bf16[2,1024]{1,0:T(2,128)(2,1)} %shard_map.82) | data formatting | bytes 8192

commit v2 on v1

--- a/solution.py
+++ b/solution.py
@@ -107,6 +107,18 @@
 def spin(values, shift):
     shift = shift % LANES
     return values if shift == 0 else pltpu.roll(values, shift, 1)
+
+
+def partner(mine, step, count):
+    if count & (count - 1):
+        return lax.rem(mine + step, count)
+    total, bit = mine, 1
+    while bit < count:
+        turn = (step // bit) % 2 if isinstance(step, int) else lax.rem(lax.div(step, bit), 2)
+        if not isinstance(turn, int) or turn:
+            total = total + turn * bit * (1 - 2 * lax.rem(lax.div(mine, bit), 2))
+        bit *= 2
+    return total
 
 
 def kernel(
@@ -208,35 +220,6 @@
             moved = [spin(tiles[part], span * (part - time)) for part in range(n_tm)]
             send_out[owner * n_tm + time] = pick_lanes(moved, lane_group).astype(jnp.bfloat16)
 
-    pl.semaphore_wait(barrier, n_dev - 1)
-
-    def out_copy(peer, slot):
-        return pltpu.make_async_remote_copy(
-            src_ref=send_out.at[peer],
-            dst_ref=recv_out.at[slot],
-            send_sem=out_send_sem.at[peer],
-            recv_sem=out_recv_sem.at[slot],
-            device_id=place(peer),
-            device_id_type=MESH,
-        )
-
-    def in_copy(peer, slot):
-        return pltpu.make_async_remote_copy(
-            src_ref=send_in.at[peer],
-            dst_ref=recv_in.at[slot],
-            send_sem=in_send_sem.at[peer],
-            recv_sem=in_recv_sem.at[slot],
-            device_id=place(peer),
-            device_id_type=MESH,
-        )
-
-    def send_first(offset, carry):
-        out_copy(lax.rem(me + offset, n_dev), me).start()
-        return carry
-
-    lax.fori_loop(1, n_dev, send_first, 0)
-    recv_out[me] = send_out[me]
-
     trans_copy.wait()
     trans_wide[...] = trans[...].astype(jnp.float32).reshape(classes * lags, LANES)
     kern[classes] = jnp.zeros((halves, SUBLANES, LANES), jnp.float32)
@@ -258,8 +241,37 @@
 
     lax.fori_loop(0, classes // SUBLANES, spread_class, 0)
 
+    pl.semaphore_wait(barrier, n_dev - 1)
+
+    def out_copy(peer, slot):
+        return pltpu.make_async_remote_copy(
+            src_ref=send_out.at[peer],
+            dst_ref=recv_out.at[slot],
+            send_sem=out_send_sem.at[peer],
+            recv_sem=out_recv_sem.at[slot],
+            device_id=place(peer),
+            device_id_type=MESH,
+        )
+
+    def in_copy(peer, slot):
+        return pltpu.make_async_remote_copy(
+            src_ref=send_in.at[peer],
+            dst_ref=recv_in.at[slot],
+            send_sem=in_send_sem.at[peer],
+            recv_sem=in_recv_sem.at[slot],
+            device_id=place(peer),
+            device_id_type=MESH,
+        )
+
+    def send_first(offset, carry):
+        out_copy(partner(me, n_dev - offset, n_dev), me).start()
+        return carry
+
+    lax.fori_loop(1, n_dev, send_first, 0)
+    recv_out[me] = send_out[me]
+
     def take_rays(step, carry):
-        owner = lax.rem(dom + step, n_dom)
+        owner = partner(dom, step, n_dom)
         for time in range(n_tm):
             slot = owner * n_tm + time
 
@@ -281,9 +293,8 @@
     lax.fori_loop(0, n_dom, take_rays, 0)
 
     def translate(step, carry):
-        owner = lax.rem(dom + step, n_dom)
-
-        def one_piece(piece, inner):
+        owner = partner(dom, n_dom - 1 - step, n_dom)
+        for piece in range(pieces):
             sums = []
             for part in range(n_tm):
                 box = owner * boxes_own + piece * n_tm + part
@@ -300,15 +311,26 @@
                     total = total + jnp.where(
                         sublane >= late, pltpu.roll(totals[half], late, 0), 0.0
                     )
-                turn = LANES // 2
-                while turn >= span:
-                    total = total + pltpu.roll(total, turn, 1)
-                    turn //= 2
                 sums.append(total)
-            rows_tmp[pl.ds(piece, SUBLANES, stride=pieces), :] = pick_lanes(sums, lane_group)
-            return inner
-
-        lax.fori_loop(0, pieces, one_piece, 0)
+            width = n_tm
+            while width > 1:
+                width //= 2
+                near = (lane_group // width) % 2 == 0
+                sums = [
+                    jnp.where(near, sums[part], sums[part + width])
+                    + pltpu.roll(
+                        jnp.where(near, sums[part + width], sums[part]), width * span, 1
+                    )
+                    if width * 2 * span == LANES
+                    else jnp.where(near, sums[part], sums[part + width])
+                    + jnp.where(
+                        near,
+                        pltpu.roll(sums[part], LANES - width * span, 1),
+                        pltpu.roll(sums[part + width], width * span, 1),
+                    )
+                    for part in range(width)
+                ]
+            rows_tmp[pl.ds(piece, SUBLANES, stride=pieces), :] = sums[0]
         for time in range(n_tm):
             slot = owner * n_tm + time
             send_in[slot] = rows_tmp[time * block : (time + 1) * block, :].astype(jnp.bfloat16)
@@ -319,12 +341,13 @@
 
         return carry
 
-    lax.fori_loop(1, n_dom + 1, translate, 0)
+    lax.fori_loop(0, n_dom, translate, 0)
     recv_in[me] = send_in[me]
 
     rec_copy.wait()
     field = jnp.zeros((rows_all, panels), jnp.float32)
-    for owner in range(n_dom):
+    for step in range(n_dom):
+        owner = partner(dom, n_dom - 1 - step, n_dom)
         tiles = []
         for time in range(n_tm):
             slot = owner * n_tm + time
@@ -341,7 +364,7 @@
         incoming = jnp.concatenate(incoming, axis=0).astype(jnp.bfloat16)
         field = field + lax.dot_general(
             incoming,
-            rec[:, owner * LANES : (owner + 1) * LANES],
+            rec[:, pl.ds(pl.multiple_of(owner * LANES, LANES), LANES)],
             (((1,), (1,)), ((), ())),
             preferred_element_type=jnp.float32,
         )

time: 26.6 us -> 23.2 us (0.87)
  Pallas kernels: 25.1 us -> 21.7 us
    pallas_call x1, Pallas kernels: 25.1 us -> 21.7 us  [fused_body(): pl.pallas_call(functools.partial(kernel, n_dom, n_tm), out_shape=jax.Shap...]
where the time goes in v2:
time: 23.2 us; the launch traced here: 23 us
  Pallas kernels  21.7 us (94%)
  local copies, waits for them, and re-layouts  1.28 us (6%)
    pallas_call x1, Pallas kernels, fused_body(): pl.pallas_call(functools.partial(kernel, n_dom, n_tm), out_shape=jax.Shap...  21.7 us
    unnamed x1, local copies, waits for them, and re-layouts  1.28 us

profile of v2, /device:TPU:0, one launch (start us, length us, event | category | flops | bytes accessed | tf_op | source)
XLA Modules:
  0.0 23.0 jit_solution(5297991271983360042)
XLA Ops:
  0.0 21.7 %shard_map.82 = bf16[2,1024]{1,0:T(2,128)(2,1)} custom-call(bf16[2,1024]{1,0:T(2,128)(2,1)} %signal_ref.1, s32[1,1024]{1,0:T(1,128)} %bitcast.3, bf16[1024,1024]{1,0:T(8,128)(2,1)} %rad_hbm.1, bf16[1024,1024]{1,0:T(8,128)(2,1)} %rec_hbm.1, bf16[64,8,128]{2,1,0:T(8,128)(2,1)} %trans_hbm.1, s32[8,128]{1,0:T(8,128)} %bitcast.4, s32[8,128]{1,0:T(8,128)} %bitcast.5, ...), custom_call_target="tpu_custom_call" | custom-call | tf_op jit(solution)/shard_map/pallas_call | solution.py:408
  21.7 1.3 %copy.10 = bf16[2,1024]{1,0:T(2,128)(2,1)} copy(bf16[2,1024]{1,0:T(2,128)(2,1)} %shard_map.82) | data formatting | bytes 8192

commit v3 on v2

--- a/solution.py
+++ b/solution.py
@@ -124,15 +124,21 @@
 def kernel(
     n_dom,
     n_tm,
-    signal_ref,
-    box_ref,
+    signal_hbm,
+    box_hbm,
     rad_hbm,
     rec_hbm,
     trans_hbm,
+    source_hbm,
+    class_hbm,
+    count_hbm,
+    out_ref,
+    signal_ref,
+    box_ref,
     source_ref,
     class_ref,
     count_ref,
-    out_ref,
+    small_sem,
     rad,
     rec,
     trans,
@@ -176,19 +182,36 @@
     rec_copy = pltpu.make_async_copy(rec_hbm, rec, load_sem.at[chunks])
     trans_copy = pltpu.make_async_copy(trans_hbm, trans, load_sem.at[chunks + 1])
 
+    barrier = pltpu.get_barrier_semaphore()
+
+    def greet(offset, carry):
+        peer = partner(me, n_dev - offset, n_dev)
+        pl.semaphore_signal(barrier, inc=1, device_id=place(peer), device_id_type=MESH)
+        return carry
+
+    small = [
+        pltpu.make_async_copy(source, target, small_sem.at[index])
+        for index, (source, target) in enumerate(
+            [
+                (signal_hbm, signal_ref),
+                (box_hbm, box_ref),
+                (source_hbm, source_ref),
+                (class_hbm, class_ref),
+                (count_hbm, count_ref),
+            ]
+        )
+    ]
+    small[0].start()
+    small[1].start()
     for index in range(chunks):
         rad_copy(index).start()
+    lax.fori_loop(1, n_dev, greet, 0)
     trans_copy.start()
+    for copy in small[2:]:
+        copy.start()
     rec_copy.start()
-
-    barrier = pltpu.get_barrier_semaphore()
-
-    def greet(offset, carry):
-        peer = lax.rem(me + offset, n_dev)
-        pl.semaphore_signal(barrier, inc=1, device_id=place(peer), device_id_type=MESH)
-        return carry
-
-    lax.fori_loop(1, n_dev, greet, 0)
+    small[0].wait()
+    small[1].wait()
 
     lane_group = lax.broadcasted_iota(jnp.int32, (SUBLANES, LANES), 1) // span
     sublane = lax.broadcasted_iota(jnp.int32, (SUBLANES, LANES), 0)
@@ -290,7 +313,10 @@
                 rays[owner * boxes_own + piece * n_tm + part] = pick_lanes(moved, lane_group)
         return carry
 
-    lax.fori_loop(0, n_dom, take_rays, 0)
+    for step in range(n_dom):
+        take_rays(step, 0)
+    for copy in small[2:]:
+        copy.wait()
 
     def translate(step, carry):
         owner = partner(dom, n_dom - 1 - step, n_dom)
@@ -402,15 +428,20 @@
     block = steps_own * (boxes_all // n_dom) // n_tm
     chunks = 4
     vmem = pl.BlockSpec(memory_space=pltpu.VMEM)
-    smem = pl.BlockSpec(memory_space=pltpu.SMEM)
     hbm = pl.BlockSpec(memory_space=pl.ANY)
     message = pltpu.VMEM((n_dev, block, LANES), jnp.bfloat16)
     return pl.pallas_call(
         functools.partial(kernel, n_dom, n_tm),
         out_shape=jax.ShapeDtypeStruct((steps_own, panels), jnp.bfloat16),
-        in_specs=[vmem, vmem, hbm, hbm, hbm, smem, smem, smem],
+        in_specs=[hbm] * 8,
         out_specs=vmem,
         scratch_shapes=[
+            pltpu.VMEM((steps_own, panels), jnp.bfloat16),
+            pltpu.VMEM((1, panels), jnp.int32),
+            pltpu.SMEM(list_source.shape[::-1], jnp.int32),
+            pltpu.SMEM(list_class.shape[::-1], jnp.int32),
+            pltpu.SMEM(list_count.shape, jnp.int32),
+            pltpu.SemaphoreType.DMA((5,)),
             pltpu.VMEM((panels, dirs_all), jnp.bfloat16),
             pltpu.VMEM((panels, dirs_all), jnp.bfloat16),
             pltpu.VMEM(translation.shape, jnp.bfloat16),

time: 23.2 us -> 22.3 us (0.961)
  Pallas kernels: 21.7 us -> 20.9 us
    pallas_call x1, Pallas kernels: 21.7 us -> 20.9 us  [fused_body(): pl.pallas_call(functools.partial(kernel, n_dom, n_tm), out_shape=jax.Shap...]
where the time goes in v3:
time: 22.3 us; the launch traced here: 22.2 us
  Pallas kernels  20.9 us (94%)
  local copies, waits for them, and re-layouts  1.28 us (6%)
    pallas_call x1, Pallas kernels, fused_body(): pl.pallas_call(functools.partial(kernel, n_dom, n_tm), out_shape=jax.Shap...  20.9 us
    unnamed x1, local copies, waits for them, and re-layouts  1.28 us

profile of v3, /device:TPU:0, one launch (start us, length us, event | category | flops | bytes accessed | tf_op | source)
XLA Modules:
  0.0 22.2 jit_solution(9683842342903110427)
XLA Ops:
  0.0 20.9 %shard_map.82 = bf16[2,1024]{1,0:T(2,128)(2,1)} custom-call(bf16[2,1024]{1,0:T(2,128)(2,1)} %signal_hbm.1, s32[1,1024]{1,0:T(1,128)} %bitcast.3, bf16[1024,1024]{1,0:T(8,128)(2,1)} %rad_hbm.1, bf16[1024,1024]{1,0:T(8,128)(2,1)} %rec_hbm.1, bf16[64,8,128]{2,1,0:T(8,128)(2,1)} %trans_hbm.1, s32[8,128]{1,0:T(8,128)} %bitcast.4, s32[8,128]{1,0:T(8,128)} %bitcast.5, ...), custom_call_target="tpu_custom_call" | custom-call | tf_op jit(solution)/shard_map/pallas_call | solution.py:433
  20.9 1.3 %copy.10 = bf16[2,1024]{1,0:T(2,128)(2,1)} copy(bf16[2,1024]{1,0:T(2,128)(2,1)} %shard_map.82) | data formatting | bytes 8192
